TPU v7x, 32 devices: a whole 2x2x4 slice. The times are simulated.
32 devices in a mesh: fiber: 2 (over x), blk: 16 (over z, y, core).
Axes of the slice: x: 2, y: 2, z: 4, core: 2. Of those that a mesh axis runs over, the one named last changes fastest.
Arguments:
- users: bfloat16 [32768, 256], P('blk', 'fiber'), may hold values from -1.5 to 1.5
- items: bfloat16 [4096, 256], P('blk'), may hold values from -1.5 to 1.5
- tile_users: int32 [16, 2, 128], P('blk', 'fiber'), may hold values from 0 to 15
- tile_items: int32 [16, 2, 128], P('blk', 'fiber'), may hold values from 0 to 31, as said below
- confidence: bfloat16 [16, 2, 128, 128, 128], P('blk', 'fiber'), may hold values from 0.19921875 to 5
Outputs:
- user_grad: bfloat16 [32768, 256], P('blk', 'fiber')
Inputs may be any that keep to these rules, and one draw needn't show every extreme that they name: `tile_items`: each device's list is sorted by item block, then user block, and holds distinct pairs; the two lists of the same index of blk share no pair. A device has at most 8 tiles in any item block, and exactly 8 in at least one.
All inputs are finite; a program needn't handle non-finite values.
Results may differ from a plain program's by a relative error of at most 0.0034.
Values may be sent and summed in bfloat16 or wider, within the bound.
No kernel may reach another device: no remote copies, remote signals or barrier semaphores. Data moves between devices by JAX's collectives and lax.ppermute only.
A program may use at most 128 MiB of HBM per device.

v0:
```python
import math
import jax
import jax.numpy as jnp
from jax import lax
from jax.sharding import PartitionSpec as P


def shards(users, items, tile_users, tile_items, confidence):
    panel_rows = lax.all_gather(users, "fiber", axis=1, tiled=True)
    tile_size = confidence.shape[-1]
    rank_width = panel_rows.shape[1]
    user_count = panel_rows.shape[0] // tile_size
    panel_blocks = panel_rows.reshape(user_count, tile_size, rank_width)
    user_list = tile_users.reshape(-1)
    item_list = tile_items.reshape(-1)
    conf_tiles = confidence.reshape(-1, tile_size, tile_size)
    tile_count = user_list.shape[0]
    item_count = items.shape[0] // tile_size * lax.axis_size("blk")
    block_ids = jnp.arange(user_count, dtype=jnp.int32)

    def accumulate(totals, user_ids, conf_part, item_rows, live_mask):
        user_rows = panel_blocks[user_ids]
        scores = jnp.einsum(
            "tar,tbr->tab", user_rows, item_rows, preferred_element_type=jnp.float32
        )
        weight = (conf_part.astype(jnp.float32) * (1.0 - scores) * live_mask[:, None, None]).astype(
            jnp.bfloat16
        )
        products = jnp.einsum("tab,tbr->tar", weight, item_rows, preferred_element_type=jnp.float32)
        return totals.at[user_ids].add(products)

    empty = jnp.zeros((user_count, tile_size, rank_width), jnp.float32)
    gathered = lax.all_gather(items, "blk", axis=0, tiled=True).reshape(
        item_count, tile_size, rank_width
    )
    group = math.gcd(tile_count, 128)
    every_live = jnp.ones((group,), jnp.float32)

    def one_group(index, running):
        first = (index * group).astype(jnp.int32)
        user_ids = lax.dynamic_slice_in_dim(user_list, first, group, 0)
        item_ids = lax.dynamic_slice_in_dim(item_list, first, group, 0)
        conf_part = lax.dynamic_slice_in_dim(conf_tiles, first, group, 0)
        return accumulate(running, user_ids, conf_part, gathered[item_ids], every_live)

    totals = lax.fori_loop(0, tile_count // group, one_group, empty)
    row_sums = jnp.sum(conf_tiles, axis=-1, dtype=jnp.float32)
    owners = (user_list[:, None] == block_ids[None, :]).astype(jnp.float32)
    row_local = jnp.einsum("tk,ta->ka", owners, row_sums, precision=lax.Precision.HIGHEST).reshape(
        -1
    )
    fiber_count = lax.axis_size("fiber")
    widened = jnp.broadcast_to(row_local[:, None], (row_local.shape[0], fiber_count))
    shares, row_total = (
        lax.psum_scatter(totals.reshape(-1, rank_width), "fiber", scatter_dimension=1, tiled=True),
        lax.psum_scatter(widened, "fiber", scatter_dimension=1, tiled=True),
    )
    return (shares * lax.rsqrt(1.0 + row_total)).astype(jnp.bfloat16)


def solution(mesh):
    in_specs = (
        P("blk", "fiber"),
        P("blk", None),
        P("blk", "fiber", None),
        P("blk", "fiber", None),
        P("blk", "fiber", None, None, None),
    )
    out_specs = P("blk", "fiber")
    return jax.shard_map(shards, mesh=mesh, in_specs=in_specs, out_specs=out_specs, check_vma=False)
```

profile of v0, /device:TPU:0, one launch (start us, length us, event | category | flops | bytes accessed | tf_op | source)
XLA Modules:
  0.0 168.0 jit_solution(1765805471388297682)
XLA Ops:
  6.5 0.0 all-gather.3.cloned.1.call-start
  6.5 0.7 all-gather.3.cloned.1.call-update
  7.3 0.0 all-gather.5.cloned.1.call-start
  7.3 0.7 all-gather.5.cloned.1.call-update
  8.0 0.0 reduce-scatter.2.cloned.1.call-start
  8.1 0.7 fusion.9
  8.7 0.7 fusion.10
  9.4 23.5 %all-gather.3.cloned.1.call-done = bf16[2048,256]{1,0:T(8,128)(2,1)} async-done(((bf16[2048,128]{1,0:T(8,128)(2,1)}), bf16[2048,256]{1,0:T(8,128)(2,1)}) %all-gather.3.cloned.1.call-update) | async-done | bytes 1048592 | tf_op jit(solution)/shard_map/all_gather | solution.py:9
  32.9 7.7 %gather_fusion = bf16[128,128,256]{2,1,0:T(8,128)(2,1)} fusion(bf16[16,128,256]{2,1,0:T(8,128)(2,1)} %bitcast.28, s32[1024]{0:T(1024)S(1)} %pad_clamp_fusion.1), kind=kCustom, calls=%fused_computation | custom fusion | bytes 16777728 | tf_op jit(solution)/shard_map/while/body/eval_jaxpr/gather | solution.py:22
  40.6 35.9 %all-gather.5.cloned.1.call-done = bf16[4096,256]{1,0:T(8,128)(2,1)} async-done(((bf16[256,256]{1,0:T(8,128)(2,1)}), bf16[4096,256]{1,0:T(8,128)(2,1)}) %all-gather.5.cloned.1.call-update) | async-done | bytes 2097168 | tf_op jit(solution)/shard_map/all_gather | solution.py:33
  76.5 8.1 %gather_fusion.1 = bf16[128,128,256]{2,1,0:T(8,128)(2,1)} fusion(bf16[32,128,256]{2,1,0:T(8,128)(2,1)} %bitcast.29, s32[1024]{0:T(1024)S(1)} %pad_clamp_fusion), kind=kCustom, calls=%fused_computation.1 | custom fusion | bytes 16777728 | tf_op jit(solution)/shard_map/while/body/eval_jaxpr/gather | solution.py:44
  84.7 17.4 %fusion.2 = f32[128,128,256]{2,1,0:T(8,128)} fusion(bf16[128,128,256]{2,1,0:T(8,128)(2,1)} %gather_fusion.1, bf16[1,1,128,128,128]{4,3,2,1,0:T(8,128)(2,1)} %param.9, bf16[128,128,256]{2,1,0:T(8,128)(2,1)} %gather_fusion), kind=kOutput, calls=%fused_computation.7 | convolution fusion | flops 2155872256 | bytes 37748736 | tf_op jit(solution)/shard_map/while/body/eval_jaxpr/tab,tbr->tar/dot_general | solution.py:29
  102.1 0.2 broadcast_in_dim.16
  102.3 0.0 copy-start.2
  102.3 0.0 copy-start.1
  102.3 24.4 %scatter_fusion = f32[16,128,256]{2,1,0:T(8,128)S(1)} fusion(f32[16,128,256]{2,1,0:T(8,128)S(1)} %broadcast_in_dim.16, s32[128]{0:T(128)S(1)} %fusion.9, f32[128,128,256]{2,1,0:T(8,128)} %fusion.2), kind=kCustom, calls=%fused_computation.2 | custom fusion | flops 4194304 | bytes 50332160 | tf_op jit(solution)/shard_map/while/body/eval_jaxpr/scatter-add | solution.py:30
  126.6 0.0 copy-start
  126.7 1.3 copy-done
  128.0 0.0 reduce-scatter.2.cloned.1.call-update
  128.0 0.0 copy-done.2
  128.0 0.6 dynamic-slice
  128.6 3.4 %convert_reduce_fusion = f32[128,128]{1,0:T(8,128)S(1)} fusion(bf16[1,1,128,128,128]{4,3,2,1,0:T(8,128)(2,1)} %param.9), kind=kLoop, calls=%fused_computation.3 | loop fusion | flops 4177920 | bytes 4259840 | tf_op jit(solution)/shard_map/reduce_sum | solution.py:47
  132.0 0.0 copy-done.1
  132.0 0.3 convolution_bitcast_fusion
  132.3 8.7 %all-reduce = f32[2048,2]{0,1:T(2,128)S(1)} all-reduce(f32[2048,2]{0,1:T(2,128)S(1)} %broadcast_in_dim.18), channel_id=3, replica_groups=mesh['fiber'=2,'blk'=16] {'fiber'}, use_global_device_ids=true, to_apply=%region_3.0.clone | all-reduce | flops 4096 | bytes 32768
  141.0 0.7 fusion.8
  141.7 17.5 %reduce-scatter.2.cloned.1.call-done = f32[2048,128]{1,0:T(8,128)} async-done(((f32[2048,256]{1,0:T(8,128)}), f32[2048,128]{1,0:T(8,128)}) %reduce-scatter.2.cloned.1.call-update) | async-done | bytes 1048592 | tf_op jit(solution)/shard_map/reduce_scatter | solution.py:55
  159.1 2.4 %multiply_convert_fusion = bf16[2048,128]{1,0:T(8,128)(2,1)} fusion(f32[2048,128]{1,0:T(8,128)} %reduce-scatter.2.cloned.1.call-done, f32[2048]{0:T(1024)S(1)} %bitcast.30), kind=kLoop, calls=%fused_computation.11 | loop fusion | flops 524288 | bytes 1581056 | tf_op jit(solution)/shard_map/convert_element_type | solution.py:58
  (3 shorter events, 0.0 us)
Async XLA Ops:
  6.5 26.3 %all-gather.3.cloned.1.call-start = ((), (), s32[]{:S(2)}) async-start(), calls=%async_computation.1 | async-start | bytes 1572864 | tf_op jit(solution)/shard_map/all_gather | solution.py:9
  7.3 69.3 %all-gather.5.cloned.1.call-start = ((), (), s32[]{:S(2)}) async-start(), calls=%async_computation.2 | async-start | bytes 2228224 | tf_op jit(solution)/shard_map/all_gather | solution.py:33
  8.0 151.1 %reduce-scatter.2.cloned.1.call-start = ((), (), s32[]{:S(2)}) async-start(), calls=%async_computation.3 | async-start | bytes 3145728 | tf_op jit(solution)/shard_map/reduce_scatter | solution.py:55
  102.3 25.8 %copy-start.2 = (u32[32]{0:T(128)S(1)}, u32[32]{0:T(128)}, u32[]{:S(2)}) copy-start(u32[32]{0:T(128)} %constant.29) | copy-start | bytes 388
  102.3 29.7 %copy-start.1 = (s32[1,1,128]{2,1,0:T(1,128)S(1)}, s32[1,1,128]{2,1,0:T(1,128)}, u32[]{:S(2)}) copy-start(s32[1,1,128]{2,1,0:T(1,128)} %param.7) | copy-start | bytes 1540
  126.6 1.3 copy-start
Sparse Core Ops, SparseCore 0:
  8.9 23.9 all-gather.2
  35.0 41.4 all-gather.4
  128.1 30.9 reduce-scatter.1
where the time goes:
time: 169 us; the launch traced here: 168 us
  waiting for transfers between devices  78.3 us (46%)
  other arithmetic  32.1 us (19%)
  local copies, waits for them, and re-layouts  18 us (11%)
  matrix products  17.7 us (10%)
  between operations  13.2 us (8%)
  blocking collectives  8.72 us (5%)
    all_gather x1, waiting for transfers between devices, shards(): lax.all_gather(items, 'blk', axis=0, tiled=True)  35.9 us
    scatter-add x1, other arithmetic, accumulate(): return totals.at[user_ids].add(products)  24.4 us
    all_gather x1, waiting for transfers between devices, shards(): panel_rows = lax.all_gather(users, 'fiber', axis=1, tiled=True)  23.5 us
    reduce_scatter x1, waiting for transfers between devices, shards(): lax.psum_scatter(totals.reshape(-1, rank_width), 'fiber', scatter_dimensi...  17.5 us
    dot_general x1, matrix products, accumulate(): jnp.einsum('tab,tbr->tar', weight, item_rows, preferred_element_type=jnp....  17.4 us
    unnamed x1, blocking collectives  8.72 us
    gather x1, local copies, waits for them, and re-layouts, one_group(): gathered[item_ids]  8.15 us
    gather x1, local copies, waits for them, and re-layouts, accumulate(): user_rows = panel_blocks[user_ids]  7.74 us
  transfers between devices with their start and end apart: 3, of which 3 were waited for; matrix products, arithmetic and copies ran while one was open for 8% of the time, Pallas kernels for 0%

commit v1 on v0

--- a/solution.py
+++ b/solution.py
@@ -6,7 +6,7 @@
 
 
 def shards(users, items, tile_users, tile_items, confidence):
-    panel_rows = lax.all_gather(users, "fiber", axis=1, tiled=True)
+    panel_rows = jnp.concatenate(lax.all_gather(users, "fiber"), axis=1)
     tile_size = confidence.shape[-1]
     rank_width = panel_rows.shape[1]
     user_count = panel_rows.shape[0] // tile_size

time: 169 us -> 168 us (level)
  transfers between devices with their start and end apart: 3 -> 3, of which waited for: 3 -> 3; matrix products, arithmetic and copies ran while one was open for 8% -> 9% of each run, Pallas kernels for 0% -> 0%
where the time goes in v1:
time: 168 us
  waiting for transfers between devices  77 us (46%)
  other arithmetic  32.1 us (19%)
  local copies, waits for them, and re-layouts  19.3 us (11%)
  matrix products  17.4 us (10%)
  between operations  13.2 us (8%)
  blocking collectives  8.71 us (5%)
    all_gather x1, waiting for transfers between devices, shards(): lax.all_gather(items, 'blk', axis=0, tiled=True)  34.6 us
    scatter-add x1, other arithmetic, accumulate(): return totals.at[user_ids].add(products)  24.4 us
    all_gather x1, waiting for transfers between devices, shards(): panel_rows = jnp.concatenate(lax.all_gather(users, 'fiber'), axis=1)  23.5 us
    reduce_scatter x1, waiting for transfers between devices, shards(): lax.psum_scatter(totals.reshape(-1, rank_width), 'fiber', scatter_dimensi...  17.5 us
    dot_general x1, matrix products, accumulate(): jnp.einsum('tab,tbr->tar', weight, item_rows, preferred_element_type=jnp....  17.1 us
    unnamed x1, blocking collectives  8.71 us
    gather x1, local copies, waits for them, and re-layouts, one_group(): gathered[item_ids]  8.16 us
    gather x1, local copies, waits for them, and re-layouts, accumulate(): user_rows = panel_blocks[user_ids]  6.53 us
  transfers between devices with their start and end apart: 3, of which 3 were waited for; matrix products, arithmetic and copies ran while one was open for 9% of the time, Pallas kernels for 0%

profile of v1, /device:TPU:0, one launch (start us, length us, event | category | flops | bytes accessed | tf_op | source)
XLA Modules:
  0.0 167.8 jit_solution(11953990467559425470)
XLA Ops:
  6.5 0.0 all-gather.6.cloned.1.call-start
  6.5 0.7 all-gather.6.cloned.1.call-update
  7.3 0.0 all-gather.4.cloned.1.call-start
  7.3 0.7 all-gather.4.cloned.1.call-update
  8.0 0.0 reduce-scatter.2.cloned.1.call-start
  8.1 0.7 fusion.9
  8.7 0.7 fusion.10
  9.4 23.5 %all-gather.6.cloned.1.call-done = bf16[4096,128]{1,0:T(8,128)(2,1)} async-done(((bf16[2048,128]{1,0:T(8,128)(2,1)}), bf16[4096,128]{1,0:T(8,128)(2,1)}) %all-gather.6.cloned.1.call-update) | async-done | bytes 1048592 | tf_op jit(solution)/shard_map/all_gather | solution.py:9
  32.9 1.5 copy.9
  34.4 0.2 copy.11
  34.6 0.8 copy.10
  35.4 6.5 %gather_fusion = bf16[128,128,256]{2,1,0:T(8,128)(2,1)} fusion(bf16[16,128,256]{2,1,0:T(8,128)(2,1)S(1)} %copy.10, s32[1024]{0:T(1024)S(1)} %pad_clamp_fusion.1), kind=kCustom, calls=%fused_computation | custom fusion | bytes 16777728 | tf_op jit(solution)/shard_map/while/body/eval_jaxpr/gather | solution.py:22
  42.0 34.6 %all-gather.4.cloned.1.call-done = bf16[4096,256]{1,0:T(8,128)(2,1)} async-done(((bf16[256,256]{1,0:T(8,128)(2,1)}), bf16[4096,256]{1,0:T(8,128)(2,1)}) %all-gather.4.cloned.1.call-update) | async-done | bytes 2097168 | tf_op jit(solution)/shard_map/all_gather | solution.py:33
  76.6 8.2 %gather_fusion.1 = bf16[128,128,256]{2,1,0:T(8,128)(2,1)} fusion(bf16[32,128,256]{2,1,0:T(8,128)(2,1)} %bitcast.34, s32[1024]{0:T(1024)S(1)} %pad_clamp_fusion), kind=kCustom, calls=%fused_computation.1 | custom fusion | bytes 16777728 | tf_op jit(solution)/shard_map/while/body/eval_jaxpr/gather | solution.py:44
  84.7 17.1 %fusion.2 = f32[128,128,256]{2,1,0:T(8,128)} fusion(bf16[128,128,256]{2,1,0:T(8,128)(2,1)} %gather_fusion.1, bf16[1,1,128,128,128]{4,3,2,1,0:T(8,128)(2,1)} %param.9, bf16[128,128,256]{2,1,0:T(8,128)(2,1)} %gather_fusion), kind=kOutput, calls=%fused_computation.7 | convolution fusion | flops 2155872256 | bytes 37748736 | tf_op jit(solution)/shard_map/while/body/eval_jaxpr/tab,tbr->tar/dot_general | solution.py:29
  101.8 0.2 broadcast_in_dim.16
  102.0 0.0 copy-start.2
  102.0 0.0 copy-start.1
  102.1 24.4 %scatter_fusion = f32[16,128,256]{2,1,0:T(8,128)S(1)} fusion(f32[16,128,256]{2,1,0:T(8,128)S(1)} %broadcast_in_dim.16, s32[128]{0:T(128)S(1)} %fusion.9, f32[128,128,256]{2,1,0:T(8,128)} %fusion.2), kind=kCustom, calls=%fused_computation.2 | custom fusion | flops 4194304 | bytes 50332160 | tf_op jit(solution)/shard_map/while/body/eval_jaxpr/scatter-add | solution.py:30
  126.4 0.0 copy-start
  126.4 1.3 copy-done
  127.8 0.0 reduce-scatter.2.cloned.1.call-update
  127.8 0.0 copy-done.2
  127.8 0.6 dynamic-slice
  128.4 3.4 %convert_reduce_fusion = f32[128,128]{1,0:T(8,128)S(1)} fusion(bf16[1,1,128,128,128]{4,3,2,1,0:T(8,128)(2,1)} %param.9), kind=kLoop, calls=%fused_computation.3 | loop fusion | flops 4177920 | bytes 4259840 | tf_op jit(solution)/shard_map/reduce_sum | solution.py:47
  131.8 0.0 copy-done.1
  131.8 0.3 convolution_bitcast_fusion
  132.1 8.7 %all-reduce = f32[2048,2]{0,1:T(2,128)S(1)} all-reduce(f32[2048,2]{0,1:T(2,128)S(1)} %broadcast_in_dim.18), channel_id=4, replica_groups=mesh['fiber'=2,'blk'=16] {'fiber'}, use_global_device_ids=true, to_apply=%region_3.0.clone | all-reduce | flops 4096 | bytes 32768
  140.8 0.7 fusion.8
  141.4 17.5 %reduce-scatter.2.cloned.1.call-done = f32[2048,128]{1,0:T(8,128)} async-done(((f32[2048,256]{1,0:T(8,128)}), f32[2048,128]{1,0:T(8,128)}) %reduce-scatter.2.cloned.1.call-update) | async-done | bytes 1048592 | tf_op jit(solution)/shard_map/reduce_scatter | solution.py:55
  158.9 2.4 %multiply_convert_fusion = bf16[2048,128]{1,0:T(8,128)(2,1)} fusion(f32[2048,128]{1,0:T(8,128)} %reduce-scatter.2.cloned.1.call-done, f32[2048]{0:T(1024)S(1)} %bitcast.38), kind=kLoop, calls=%fused_computation.11 | loop fusion | flops 524288 | bytes 1581056 | tf_op jit(solution)/shard_map/convert_element_type | solution.py:58
  (3 shorter events, 0.0 us)
Async XLA Ops:
  6.5 26.4 %all-gather.6.cloned.1.call-start = ((), (), s32[]{:S(2)}) async-start(), calls=%async_computation.3 | async-start | bytes 1572864 | tf_op jit(solution)/shard_map/all_gather | solution.py:9
  7.3 69.3 %all-gather.4.cloned.1.call-start = ((), (), s32[]{:S(2)}) async-start(), calls=%async_computation.1 | async-start | bytes 2228224 | tf_op jit(solution)/shard_map/all_gather | solution.py:33
  8.0 150.9 %reduce-scatter.2.cloned.1.call-start = ((), (), s32[]{:S(2)}) async-start(), calls=%async_computation.2 | async-start | bytes 3145728 | tf_op jit(solution)/shard_map/reduce_scatter | solution.py:55
  102.0 25.8 %copy-start.2 = (u32[32]{0:T(128)S(1)}, u32[32]{0:T(128)}, u32[]{:S(2)}) copy-start(u32[32]{0:T(128)} %constant.29) | copy-start | bytes 388
  102.0 29.7 %copy-start.1 = (s32[1,1,128]{2,1,0:T(1,128)S(1)}, s32[1,1,128]{2,1,0:T(1,128)}, u32[]{:S(2)}) copy-start(s32[1,1,128]{2,1,0:T(1,128)} %param.7) | copy-start | bytes 1540
  126.4 1.3 copy-start
Sparse Core Ops, SparseCore 0:
  8.9 23.9 all-gather.5
  35.1 41.4 all-gather.3
  127.9 30.9 reduce-scatter.1
